TPU v7x, 256 devices: a whole 4x4x8 slice. The times are simulated.
256 devices in a mesh: wide: 32 (over x, y, core), narrow: 8 (over z).
Axes of the slice: x: 4, y: 4, z: 8, core: 2. Of those that a mesh axis runs over, the one named last changes fastest.
Arguments:
- sources: float32 [32, 8, 16, 2, 512], P('wide', 'narrow'), may hold values from -6 to 6
- schur_blocks: bfloat16 [32, 8, 2048, 2048], P('wide', 'narrow'), as said below
- scaling: float32 [32, 8, 2, 512], P('wide', 'narrow'), may hold values from 0.08 to 0.4
- coarse_basis: float32 [32, 8, 2, 2, 8, 512], P('wide', 'narrow'), may hold values from -0.09375 to 0.09375
- coarse_inverse: float32 [32, 80, 80], P('wide'), as said below
- face_sizes: int32 [32, 8, 2], P('wide', 'narrow'), may hold values from 0 to 512, as said below
- face_match: int32 [32, 8, 2, 512], P('wide', 'narrow'), may hold values from 0 to 511, as said below
- face_slots: int32 [32, 8, 4], P('wide', 'narrow'), may hold values from 0 to 3, each once within a row
- corner_slots: int32 [33, 9], replicated, may hold values from 0 to 319, as said below
Outputs:
- solution: float32 [32, 8, 16, 2, 512], P('wide', 'narrow')
- residual: float32 [32, 8, 16, 2, 512], P('wide', 'narrow')
Inputs may be any that keep to these rules, and one draw needn't show every extreme that they name: `face_sizes`: the east faces of the last wide index and the north faces of the last narrow index have 0 unknowns; every other face has 128 to 512, and some face has exactly 512. `face_match`: each block is a permutation of 0 to 511 that maps the positions below the size of the matching owned face onto themselves. `corner_slots`: distinct slots for distinct vertices; slot 319 is used. `schur_blocks`: each block is symmetric and positive definite. `coarse_inverse`: each block is symmetric and positive definite.
All inputs are finite; a program needn't handle non-finite values.
Results may differ from a plain program's by a relative error of at most 0.0052.
Values may be sent and summed in bfloat16 or wider, within the bound.
A program may use at most 64 MiB of HBM per device.

v0:
```python
import jax
import jax.numpy as jnp
from jax import lax
from jax.sharding import PartitionSpec as P

ITERS = 2
highest = lax.Precision.HIGHEST


def shifted(block, axis, distance):
    devices = range(lax.axis_size(axis))
    route = [(i - distance, i) for i in devices if i - distance in devices]
    return lax.ppermute(block, axis, route)


def body(
    sources,
    schur_blocks,
    scaling,
    coarse_basis,
    coarse_inverse,
    face_sizes,
    face_match,
    face_slots,
    corner_slots,
):
    wide_count = lax.axis_size("wide")
    wide_at = lax.axis_index("wide")
    narrow_at = lax.axis_index("narrow")
    nrhs_count = sources.shape[2]
    face_width = sources.shape[4]
    basis_count = coarse_basis.shape[4]
    block_order = coarse_inverse.shape[1]
    capacity = block_order // basis_count
    slot_count = capacity * wide_count
    places = lax.broadcasted_iota(jnp.int32, (2, face_width), 1)
    live_mask = (places < face_sizes[0, 0][:, None]).astype(jnp.float32)
    weights = scaling[0, 0] * live_mask
    vectors = coarse_basis[0, 0] * live_mask[:, None, None, :]
    forward = face_match[0, 0]
    source_rows = lax.broadcasted_iota(jnp.int32, (2, face_width, face_width), 1)
    match_table = (forward[:, None, :] == source_rows).astype(jnp.float32)
    match_narrow = match_table.astype(jnp.bfloat16)
    slot_table = (face_slots[0, 0][:, None] == jnp.arange(4, dtype=jnp.int32)[None, :]).astype(
        jnp.float32
    )
    matrix = schur_blocks[0, 0]
    square = lax.dynamic_slice(corner_slots, (wide_at, narrow_at), (2, 2))
    corner_ids = jnp.stack([square[1, 0], square[1, 1], square[0, 1], square[1, 1]])
    incidence = (corner_ids[:, None] == jnp.arange(slot_count, dtype=jnp.int32)[None, :]).astype(
        jnp.float32
    )
    inverse_block = coarse_inverse[0]
    initial = sources[0, 0] * live_mask[None]

    def finish(residual, solved_slots):
        local_values = jnp.dot(
            incidence, solved_slots, precision=highest, preferred_element_type=jnp.float32
        )
        local_values = local_values.reshape(2, 2, basis_count, nrhs_count)
        return weights[None] * residual + jnp.einsum(
            "femk,femr->rfk", vectors, local_values, precision=highest
        )

    def precondition(residual):
        partial_value = jnp.einsum("femk,rfk->femr", vectors, residual, precision=highest).reshape(
            4, basis_count * nrhs_count
        )
        dense_part = jnp.dot(
            incidence.T, partial_value, precision=highest, preferred_element_type=jnp.float32
        )
        owned_rows = lax.psum_scatter(dense_part, "wide", scatter_dimension=0, tiled=True)
        owner_block = lax.psum(owned_rows, "narrow").reshape(block_order, nrhs_count)
        solved = jnp.dot(
            inverse_block, owner_block, precision=highest, preferred_element_type=jnp.float32
        )
        all_solved = lax.all_gather(
            solved.reshape(capacity, basis_count * nrhs_count), "wide", axis=0, tiled=True
        )
        precond = finish(residual, all_solved)
        inner_value = lax.psum(jnp.sum(residual * precond, axis=(1, 2)), ("wide", "narrow"))
        return (precond, inner_value)

    residual = initial
    solution = jnp.zeros_like(initial)
    precond, inner_now = precondition(residual)
    direction = precond
    for iteration in range(ITERS):
        rounded = direction.astype(jnp.bfloat16)
        from_west = shifted(rounded[:, 0], "wide", 1)
        from_south = shifted(rounded[:, 1], "narrow", 1)
        west_face = jnp.dot(from_west, match_narrow[0], preferred_element_type=jnp.float32)
        south_face = jnp.dot(from_south, match_narrow[1], preferred_element_type=jnp.float32)
        stacked = jnp.stack(
            [
                rounded[:, 0].astype(jnp.float32),
                rounded[:, 1].astype(jnp.float32),
                west_face,
                south_face,
            ],
            axis=1,
        )
        slotted = jnp.einsum("rdk,ds->rsk", stacked, slot_table, precision=highest).astype(
            jnp.bfloat16
        )
        product = jnp.dot(
            slotted.reshape(nrhs_count, 4 * face_width), matrix, preferred_element_type=jnp.float32
        )
        by_face = jnp.einsum(
            "rsk,ds->rdk", product.reshape(nrhs_count, 4, face_width), slot_table, precision=highest
        )
        to_west = jnp.einsum("rk,mk->rm", by_face[:, 2], match_table[0], precision=highest)
        to_south = jnp.einsum("rk,mk->rm", by_face[:, 3], match_table[1], precision=highest)
        from_east = shifted(to_west, "wide", -1)
        from_north = shifted(to_south, "narrow", -1)
        summed_all = jnp.stack([by_face[:, 0] + from_east, by_face[:, 1] + from_north], axis=1)
        applied = summed_all * live_mask[None]
        curvature = lax.psum(jnp.sum(direction * applied, axis=(1, 2)), ("wide", "narrow"))
        step_size = inner_now / curvature
        solution = solution + step_size[:, None, None] * direction
        residual = residual - step_size[:, None, None] * applied
        if iteration + 1 < ITERS:
            precond, inner_new = precondition(residual)
            direction = precond + (inner_new / inner_now)[:, None, None] * direction
            inner_now = inner_new
    return (solution[None, None], residual[None, None])


def solution(mesh):
    placed = (
        P("wide", "narrow", None, None, None),
        P("wide", "narrow", None, None),
        P("wide", "narrow", None, None),
        P("wide", "narrow", None, None, None, None),
        P("wide", None, None),
        P("wide", "narrow", None),
        P("wide", "narrow", None, None),
        P("wide", "narrow", None),
        P(),
    )
    return jax.shard_map(
        body,
        mesh=mesh,
        in_specs=placed,
        out_specs=(P("wide", "narrow", None, None, None), P("wide", "narrow", None, None, None)),
        check_vma=False,
    )
```

profile of v0, /device:TPU:1, one launch (start us, length us, event | category | flops | bytes accessed | tf_op | source)
XLA Modules:
  0.0 640.1 jit_solution(5082868968421109135)
XLA Ops:
  7.2 0.8 dynamic_slice.3
  8.0 0.7 fusion.58
  8.7 0.7 fusion.47
  9.4 1.1 fusion.22
  10.6 2.1 pad_add_fusion
  12.6 1.1 fusion.46
  13.8 0.8 bitcast_select_fusion
  14.5 1.3 dynamic-slice
  16.4 110.0 %all-reduce.6.cloned.1.call-done = f32[320,128]{1,0:T(8,128)} async-done(((f32[320,128]{1,0:T(8,128)}), f32[320,128]{1,0:T(8,128)}) %all-reduce.6.cloned.1.call-update) | async-done | bytes 163856
  126.4 0.7 constant_dynamic-slice_fusion.1
  127.2 23.5 %psum.42 = f32[80,16]{1,0:T(8,128)S(1)} all-reduce(f32[80,16]{1,0:T(8,128)S(1)} %reshape.170), channel_id=1, replica_groups=mesh['wide'=32,'narrow'=8] {'narrow'}, use_global_device_ids=true, to_apply=%region_1.0 | all-reduce | flops 1280 | bytes 10240 | tf_op jit(solution)/shard_map/psum | solution.py:73
  151.1 30.1 %all-gather = f32[32,10,128]{2,1,0:T(8,128)S(1)} all-gather(f32[1,10,128]{2,1,0:T(8,128)S(1)} %reshape.179), channel_id=1, replica_groups=mesh['wide'=32,'narrow'=8] {'wide'}, dimensions={0}, use_global_device_ids=true | all-gather | bytes 168960 | tf_op jit(solution)/shard_map/all_gather | solution.py:77
  181.6 1.1 fusion.59
  182.7 1.3 collective-permute-start.1
  184.1 1.2 convert_convert_fusion
  185.3 12.3 %copy.57 = bf16[2048,2048]{1,0:T(8,128)(2,1)} copy(bf16[2048,2048]{0,1:T(8,128)(2,1)} %bitcast.206) | data formatting | bytes 16777216 | tf_op jit(solution)/shard_map/dot_general | solution.py:106
  197.6 2.6 collective-permute-start
  200.4 0.7 collective-permute-done
  201.2 0.4 fusion
  201.7 5.6 fusion.60
  207.8 0.5 fusion.5
  208.3 0.6 fusion.7
  208.9 1.3 collective-permute-start.3
  210.2 1.9 collective-permute-start.2
  212.1 2.1 collective-permute-done.3
  214.2 1.7 collective-permute-done.2
  216.1 78.5 %all-reduce.2 = (f32[16]{0:T(128)S(1)}, f32[16]{0:T(128)S(1)}) all-reduce(f32[16]{0:T(128)S(1)} %get-tuple-element.9, f32[16]{0:T(128)S(1)} %get-tuple-element.8), channel_id=1, replica_groups=mesh['wide'=32,'narrow'=8] {'wide','narrow'}, use_global_device_ids=true, to_apply=%region_3.0 | all-reduce | flops 32 | bytes 256 | tf_op jit(solution)/shard_map/psum | solution.py:81
  295.0 1.1 fusion.44
  296.1 106.8 %all-reduce.8.cloned.1.call-done = f32[320,128]{1,0:T(8,128)} async-done(((f32[320,128]{1,0:T(8,128)}), f32[320,128]{1,0:T(8,128)}) %all-reduce.8.cloned.1.call-update) | async-done | bytes 163856
  402.9 0.7 constant_dynamic-slice_fusion
  403.7 23.5 %psum.45 = f32[80,16]{1,0:T(8,128)S(1)} all-reduce(f32[80,16]{1,0:T(8,128)S(1)} %reshape.175), channel_id=1, replica_groups=mesh['wide'=32,'narrow'=8] {'narrow'}, use_global_device_ids=true, to_apply=%region_7.0 | all-reduce | flops 1280 | bytes 10240 | tf_op jit(solution)/shard_map/psum | solution.py:73
  427.6 30.1 %all-gather.1 = f32[32,10,128]{2,1,0:T(8,128)S(1)} all-gather(f32[1,10,128]{2,1,0:T(8,128)S(1)} %reshape.181), channel_id=1, replica_groups=mesh['wide'=32,'narrow'=8] {'wide'}, dimensions={0}, use_global_device_ids=true | all-gather | bytes 168960 | tf_op jit(solution)/shard_map/all_gather | solution.py:77
  458.1 0.4 multiply_reduce_fusion
  458.5 73.3 %psum.46 = f32[16]{0:T(128)S(1)} all-reduce(f32[16]{0:T(128)S(1)} %get-tuple-element.39), channel_id=1, replica_groups=mesh['wide'=32,'narrow'=8] {'wide','narrow'}, use_global_device_ids=true, to_apply=%region_9.0 | all-reduce | flops 16 | bytes 128 | tf_op jit(solution)/shard_map/psum | solution.py:81
  531.9 2.4 collective-permute-start.4
  534.4 3.9 collective-permute-start.5
  538.4 0.5 collective-permute-done.5
  539.1 0.4 fusion.1
  539.5 5.6 fusion.61
  545.6 0.5 fusion.4
  546.1 0.6 fusion.6
  546.7 1.3 collective-permute-start.7
  548.0 2.7 collective-permute-start.6
  550.8 0.9 collective-permute-done.7
  551.6 1.6 collective-permute-done.6
  553.5 78.3 %psum.47 = f32[16]{0:T(128)S(1)} all-reduce(f32[16]{0:T(128)S(1)} %fusion.15), channel_id=1, replica_groups=mesh['wide'=32,'narrow'=8] {'wide','narrow'}, use_global_device_ids=true, to_apply=%region_11.0 | all-reduce | flops 16 | bytes 128 | tf_op jit(solution)/shard_map/psum | solution.py:118
  631.8 0.7 copy.47
  632.6 0.7 copy.48
  (55 shorter events, 4.3 us)
Async XLA Ops:
  7.2 143.6 %copy-start = (f32[1,80,80]{2,1,0:T(8,128)S(1)}, f32[1,80,80]{2,1,0:T(8,128)}, u32[]{:S(2)}) copy-start(f32[1,80,80]{2,1,0:T(8,128)} %param.13) | copy-start | bytes 76804
  7.2 119.2 %all-reduce.6.cloned.1.call-start = ((), (), s32[]{:S(2)}) async-start(), calls=%async_computation | async-start | bytes 327680
  13.7 389.2 %all-reduce.8.cloned.1.call-start = ((), (), s32[]{:S(2)}) async-start(), calls=%async_computation.1 | async-start | bytes 327680
  182.7 17.5 %collective-permute-start.1 = (bf16[16,512]{1,0:T(8,128)(2,1)S(1)}, bf16[16,512]{1,0:T(8,128)(2,1)S(1)}, u32[]{:S(2)}, u32[]{:S(2)}) collective-permute-start(bf16[16,512]{1,0:T(8,128)(2,1)S(1)} %get-tuple-element.30), channel_id=1, source_target_pairs={{0,1},{1,2},{2,3},{3,4},{4,5},{5,6},{6,7},{8,9},{9,10},{10,11},{11... | collective-permute-start | bytes 49160 | tf_op jit(solution)/shard_map/ppermute | solution.py:13
  185.3 16.0 %copy-start.3 = (s32[1,1,4]{2,1,0:T(1,128)S(1)}, s32[1,1,4]{2,1,0:T(1,128)}, u32[]{:S(2)}) copy-start(s32[1,1,4]{2,1,0:T(1,128)} %param.16) | copy-start | bytes 52
  197.6 18.4 %copy-start.1 = (f32[1,1,16,2,512]{4,3,2,1,0:T(2,128)S(1)}, f32[1,1,16,2,512]{4,3,2,1,0:T(2,128)}, u32[]{:S(2)}) copy-start(f32[1,1,16,2,512]{4,3,2,1,0:T(2,128)} %param.9) | copy-start | bytes 196612
  197.6 97.1 %copy-start.2 = (f32[1,1,2,2,8,512]{5,4,3,2,1,0:T(8,128)S(1)}, f32[1,1,2,2,8,512]{5,4,3,2,1,0:T(8,128)}, u32[]{:S(2)}) copy-start(f32[1,1,2,2,8,512]{5,4,3,2,1,0:T(8,128)} %param.12) | copy-start | bytes 196612
  197.6 3.4 collective-permute-start
  208.9 5.4 collective-permute-start.3
  210.2 5.8 collective-permute-start.2
  531.9 6.3 collective-permute-start.4
  534.4 4.5 collective-permute-start.5
  546.7 4.9 collective-permute-start.7
  548.0 5.2 collective-permute-start.6
Sparse Core Ops, SparseCore 0:
  13.8 112.5 all-reduce.5
  296.3 106.6 all-reduce.7
where the time goes:
time: 641 us; the launch traced here: 640 us
  blocking collectives  337 us (53%)
  waiting for transfers between devices  224 us (35%)
  matrix products  21.5 us (3%)
  local copies, waits for them, and re-layouts  18.9 us (3%)
  starting transfers between devices  17.5 us (3%)
  between operations  15 us (2%)
    unnamed x4, waiting for transfers between devices  217 us
    psum x2, blocking collectives, precondition(): lax.psum(jnp.sum(residual * precond, axis=(1, 2)), ('wide', 'narrow'))  152 us
    psum x1, blocking collectives, body(): lax.psum(jnp.sum(direction * applied, axis=(1, 2)), ('wide', 'narrow'))  78.3 us
    all_gather x2, blocking collectives, precondition(): lax.all_gather(solved.reshape(capacity, basis_count * nrhs_count), 'wide'...  60.2 us
    psum x2, blocking collectives, precondition(): lax.psum(owned_rows, 'narrow').reshape(block_order, nrhs_count)  47.1 us
    ppermute x8, starting transfers between devices, shifted(): return lax.ppermute(block, axis, route)  17.5 us
  transfers between devices with their start and end apart: 10, of which 8 were waited for; matrix products, arithmetic and copies ran while one was open for 2% of the time, Pallas kernels for 0%

commit v1 on v0

--- a/solution.py
+++ b/solution.py
@@ -78,7 +78,7 @@
             solved.reshape(capacity, basis_count * nrhs_count), "wide", axis=0, tiled=True
         )
         precond = finish(residual, all_solved)
-        inner_value = lax.psum(jnp.sum(residual * precond, axis=(1, 2)), ("wide", "narrow"))
+        inner_value = lax.psum(lax.psum(jnp.sum(residual * precond, axis=(1, 2)), "narrow"), "wide")
         return (precond, inner_value)
 
     residual = initial

time: 641 us -> 716 us (1.12)
  blocking collectives: 337 us -> 415 us
    psum x1 -> x2, blocking collectives: 78.3 us -> 154 us  [body(): lax.psum(jnp.sum(direction * applied, axis=(1, 2)), ('wide', 'narrow'))]
    psum x2 -> x4, blocking collectives: 152 us -> 154 us  [the longest x2 129 us: precondition(): lax.psum(lax.psum(jnp.sum(residual * precond, axis=(1, 2)), 'narrow'), 'w...]
where the time goes in v1:
time: 716 us; the launch traced here: 715 us
  blocking collectives  415 us (58%)
  waiting for transfers between devices  222 us (31%)
  matrix products  21.5 us (3%)
  local copies, waits for them, and re-layouts  18.9 us (3%)
  starting transfers between devices  16.6 us (2%)
  between operations  15 us (2%)
    unnamed x4, waiting for transfers between devices  215 us
    psum x2, blocking collectives, body(): lax.psum(jnp.sum(direction * applied, axis=(1, 2)), ('wide', 'narrow'))  154 us
    psum x2, blocking collectives, precondition(): lax.psum(lax.psum(jnp.sum(residual * precond, axis=(1, 2)), 'narrow'), 'w...  129 us
    all_gather x2, blocking collectives, precondition(): lax.all_gather(solved.reshape(capacity, basis_count * nrhs_count), 'wide'...  60.2 us
    psum x2, blocking collectives, precondition(): lax.psum(owned_rows, 'narrow').reshape(block_order, nrhs_count)  47.1 us
    psum x2, blocking collectives, precondition(): lax.psum(jnp.sum(residual * precond, axis=(1, 2)), 'narrow')  25.7 us
    ppermute x8, starting transfers between devices, shifted(): return lax.ppermute(block, axis, route)  16.5 us
  transfers between devices with their start and end apart: 10, of which 8 were waited for; matrix products, arithmetic and copies ran while one was open for 2% of the time, Pallas kernels for 0%

profile of v1, /device:TPU:1, one launch (start us, length us, event | category | flops | bytes accessed | tf_op | source)
XLA Modules:
  0.0 715.2 jit_solution(7133681904854708916)
XLA Ops:
  7.2 0.8 dynamic_slice.3
  8.0 0.7 fusion.58
  8.7 0.7 fusion.47
  9.4 1.1 fusion.22
  10.6 2.1 pad_add_fusion
  12.6 1.1 fusion.46
  13.8 0.8 bitcast_select_fusion
  14.5 1.3 dynamic-slice
  16.4 110.0 %all-reduce.5.cloned.1.call-done = f32[320,128]{1,0:T(8,128)} async-done(((f32[320,128]{1,0:T(8,128)}), f32[320,128]{1,0:T(8,128)}) %all-reduce.5.cloned.1.call-update) | async-done | bytes 163856
  126.4 0.7 constant_dynamic-slice_fusion.1
  127.2 23.5 %psum.56 = f32[80,16]{1,0:T(8,128)S(1)} all-reduce(f32[80,16]{1,0:T(8,128)S(1)} %reshape.170), channel_id=1, replica_groups=mesh['wide'=32,'narrow'=8] {'narrow'}, use_global_device_ids=true, to_apply=%region_1.0 | all-reduce | flops 1280 | bytes 10240 | tf_op jit(solution)/shard_map/psum | solution.py:73
  151.1 30.1 %all-gather = f32[32,10,128]{2,1,0:T(8,128)S(1)} all-gather(f32[1,10,128]{2,1,0:T(8,128)S(1)} %reshape.179), channel_id=1, replica_groups=mesh['wide'=32,'narrow'=8] {'wide'}, dimensions={0}, use_global_device_ids=true | all-gather | bytes 168960 | tf_op jit(solution)/shard_map/all_gather | solution.py:77
  181.6 1.1 fusion.59
  182.7 1.3 collective-permute-start.1
  184.1 1.2 convert_convert_fusion
  185.3 12.3 %copy.57 = bf16[2048,2048]{1,0:T(8,128)(2,1)} copy(bf16[2048,2048]{0,1:T(8,128)(2,1)} %bitcast.206) | data formatting | bytes 16777216 | tf_op jit(solution)/shard_map/dot_general | solution.py:106
  197.6 2.6 collective-permute-start
  200.4 0.7 collective-permute-done
  201.3 0.4 fusion
  201.7 5.6 fusion.60
  207.8 0.5 fusion.5
  208.3 0.6 fusion.7
  208.9 1.3 collective-permute-start.3
  210.2 1.9 collective-permute-start.2
  212.1 2.1 collective-permute-done.3
  214.2 1.7 collective-permute-done.2
  216.1 14.2 %psum.57 = f32[16]{0:T(128)S(1)} all-reduce(f32[16]{0:T(128)S(1)} %get-tuple-element.9), channel_id=1, replica_groups=mesh['wide'=32,'narrow'=8] {'narrow'}, use_global_device_ids=true, to_apply=%region_3.0 | all-reduce | flops 16 | bytes 128 | tf_op jit(solution)/shard_map/psum | solution.py:81
  230.4 78.1 %psum.59 = f32[16]{0:T(128)S(1)} all-reduce(f32[16]{0:T(128)S(1)} %get-tuple-element.8), channel_id=1, replica_groups=mesh['wide'=32,'narrow'=8] {'wide','narrow'}, use_global_device_ids=true, to_apply=%region_6.0 | all-reduce | flops 16 | bytes 128 | tf_op jit(solution)/shard_map/psum | solution.py:118
  308.5 62.9 %psum.58 = f32[16]{0:T(128)S(1)} all-reduce(f32[16]{0:T(128)S(1)} %psum.57), channel_id=1, replica_groups=mesh['wide'=32,'narrow'=8] {'wide'}, use_global_device_ids=true, to_apply=%region_4.0 | all-reduce | flops 16 | bytes 128 | tf_op jit(solution)/shard_map/psum | solution.py:81
  371.8 1.1 fusion.44
  372.9 105.1 %all-reduce.7.cloned.1.call-done = f32[320,128]{1,0:T(8,128)} async-done(((f32[320,128]{1,0:T(8,128)}), f32[320,128]{1,0:T(8,128)}) %all-reduce.7.cloned.1.call-update) | async-done | bytes 163856
  478.0 0.7 constant_dynamic-slice_fusion
  478.8 23.5 %psum.60 = f32[80,16]{1,0:T(8,128)S(1)} all-reduce(f32[80,16]{1,0:T(8,128)S(1)} %reshape.175), channel_id=1, replica_groups=mesh['wide'=32,'narrow'=8] {'narrow'}, use_global_device_ids=true, to_apply=%region_8.0 | all-reduce | flops 1280 | bytes 10240 | tf_op jit(solution)/shard_map/psum | solution.py:73
  502.8 30.1 %all-gather.1 = f32[32,10,128]{2,1,0:T(8,128)S(1)} all-gather(f32[1,10,128]{2,1,0:T(8,128)S(1)} %reshape.181), channel_id=1, replica_groups=mesh['wide'=32,'narrow'=8] {'wide'}, dimensions={0}, use_global_device_ids=true | all-gather | bytes 168960 | tf_op jit(solution)/shard_map/all_gather | solution.py:77
  533.6 11.5 %psum.61 = f32[16]{0:T(128)S(1)} all-reduce(f32[16]{0:T(128)S(1)} %get-tuple-element.37), channel_id=1, replica_groups=mesh['wide'=32,'narrow'=8] {'narrow'}, use_global_device_ids=true, to_apply=%region_10.0 | all-reduce | flops 16 | bytes 128 | tf_op jit(solution)/shard_map/psum | solution.py:81
  545.0 65.8 %psum.62 = f32[16]{0:T(128)S(1)} all-reduce(f32[16]{0:T(128)S(1)} %psum.61), channel_id=1, replica_groups=mesh['wide'=32,'narrow'=8] {'wide'}, use_global_device_ids=true, to_apply=%region_11.0 | all-reduce | flops 16 | bytes 128 | tf_op jit(solution)/shard_map/psum | solution.py:81
  610.9 1.9 collective-permute-start.4
  612.8 2.9 collective-permute-start.5
  616.0 0.5 collective-permute-done.5
  617.1 5.6 fusion.61
  623.1 0.5 fusion.4
  623.7 0.6 fusion.6
  624.2 1.3 collective-permute-start.7
  625.6 3.3 collective-permute-start.6
  629.2 1.9 collective-permute-done.6
  631.3 75.5 %psum.63 = f32[16]{0:T(128)S(1)} all-reduce(f32[16]{0:T(128)S(1)} %fusion.15), channel_id=1, replica_groups=mesh['wide'=32,'narrow'=8] {'wide','narrow'}, use_global_device_ids=true, to_apply=%region_13.0 | all-reduce | flops 16 | bytes 128 | tf_op jit(solution)/shard_map/psum | solution.py:118
  706.9 0.7 copy.47
  707.6 0.7 copy.48
  (58 shorter events, 5.5 us)
Async XLA Ops:
  7.2 143.6 %copy-start = (f32[1,80,80]{2,1,0:T(8,128)S(1)}, f32[1,80,80]{2,1,0:T(8,128)}, u32[]{:S(2)}) copy-start(f32[1,80,80]{2,1,0:T(8,128)} %param.13) | copy-start | bytes 76804
  7.2 119.2 %all-reduce.5.cloned.1.call-start = ((), (), s32[]{:S(2)}) async-start(), calls=%async_computation | async-start | bytes 327680
  13.7 464.3 %all-reduce.7.cloned.1.call-start = ((), (), s32[]{:S(2)}) async-start(), calls=%async_computation.1 | async-start | bytes 327680
  182.7 17.5 %collective-permute-start.1 = (bf16[16,512]{1,0:T(8,128)(2,1)S(1)}, bf16[16,512]{1,0:T(8,128)(2,1)S(1)}, u32[]{:S(2)}, u32[]{:S(2)}) collective-permute-start(bf16[16,512]{1,0:T(8,128)(2,1)S(1)} %get-tuple-element.28), channel_id=1, source_target_pairs={{0,1},{1,2},{2,3},{3,4},{4,5},{5,6},{6,7},{8,9},{9,10},{10,11},{11... | collective-permute-start | bytes 49160 | tf_op jit(solution)/shard_map/ppermute | solution.py:13
  185.3 16.0 %copy-start.3 = (s32[1,1,4]{2,1,0:T(1,128)S(1)}, s32[1,1,4]{2,1,0:T(1,128)}, u32[]{:S(2)}) copy-start(s32[1,1,4]{2,1,0:T(1,128)} %param.16) | copy-start | bytes 52
  197.6 18.4 %copy-start.1 = (f32[1,1,16,2,512]{4,3,2,1,0:T(2,128)S(1)}, f32[1,1,16,2,512]{4,3,2,1,0:T(2,128)}, u32[]{:S(2)}) copy-start(f32[1,1,16,2,512]{4,3,2,1,0:T(2,128)} %param.9) | copy-start | bytes 196612
  197.6 173.8 %copy-start.2 = (f32[1,1,2,2,8,512]{5,4,3,2,1,0:T(8,128)S(1)}, f32[1,1,2,2,8,512]{5,4,3,2,1,0:T(8,128)}, u32[]{:S(2)}) copy-start(f32[1,1,2,2,8,512]{5,4,3,2,1,0:T(8,128)} %param.12) | copy-start | bytes 196612
  197.6 3.4 collective-permute-start
  208.9 5.4 collective-permute-start.3
  210.2 5.8 collective-permute-start.2
  610.9 4.9 collective-permute-start.4
  612.8 3.6 collective-permute-start.5
  624.2 4.9 collective-permute-start.7
  625.6 5.5 collective-permute-start.6
Sparse Core Ops, SparseCore 0:
  13.8 112.5 all-reduce.4
  373.0 104.9 all-reduce.6
